TPU v7x, 512 devices: a whole 4x8x8 slice. The times are simulated.
512 devices in a mesh: grp: 8 (over y), tm: 64 (over z, x, core).
Axes of the slice: x: 4, y: 8, z: 8, core: 2. Of those that a mesh axis runs over, the one named last changes fastest.
Arguments:
- audio_rows: bfloat16 [131072, 1024], P(('grp', 'tm')), may hold values from -6 to 6
- routing: int32 [131072, 1], P(('grp', 'tm')), may hold values from 0 to 63; in each aligned block of 256 rows (0 to 255, 256 to 511, ...) at most 8 rows name the same one
- row_band: int32 [131072], P(('grp', 'tm')), may hold values from 0 to 3
- block_band: int32 [512], P(('grp', 'tm')), may hold values from 0 to 3
- latents: bfloat16 [65536, 1024], P(('grp', 'tm')), may hold values from -480 to 480
- kv_weight: bfloat16 [1024, 2048], P('tm'), may hold values from -0.1875 to 0.1875
- null_key: float32 [1024], replicated, may hold values from -6 to 6
- null_value: float32 [1024], replicated, may hold values from -6 to 6
- out_weight: bfloat16 [1024, 1024], replicated, may hold values from -0.1875 to 0.1875
- mlp_gain: float32 [1024], replicated, may hold values from 0.25 to 1.75
- up_weight: bfloat16 [1024, 8192], P('tm', 'grp'), may hold values from -0.1875 to 0.1875
- down_weight: bfloat16 [8192, 1024], P('grp', 'tm'), may hold values from -0.25 to 0.25
Outputs:
- mixed: bfloat16 [65536, 1024], P('tm', 'grp')
Inputs may be any that keep to these rules, and one draw needn't show every extreme that they name: `routing`: among the rows of one device no window is named by more than 8 rows, and in some devices' rows one window is named by exactly 8.
All inputs are finite; a program needn't handle non-finite values.
Results may differ from a plain program's by a relative error of at most 0.015.
Values may be sent and summed in bfloat16 or wider, within the bound.
No kernel may reach another device: no remote copies, remote signals or barrier semaphores. Data moves between devices by JAX's collectives and lax.ppermute only.
A program may use at most 64 MiB of HBM per device.

v0:
```python
import jax
import jax.numpy as jnp
from jax import lax
from jax.sharding import PartitionSpec as P

HD = 128


def attend(queries, kv_slots, usable, null_key, null_value):
    count = queries.shape[0]
    slots = kv_slots.shape[0]
    width = queries.shape[1]
    heads = width // HD
    scale = 1.0 / float(HD) ** 0.5
    query = queries.reshape(count, heads, HD)
    keyset = kv_slots[:, :width].reshape(slots, heads, HD)
    valset = kv_slots[:, width:].reshape(slots, heads, HD)
    scores = jnp.einsum("lhd,shd->hls", query, keyset, preferred_element_type=jnp.float32) * scale
    null_scores = (
        jnp.einsum("lhd,hd->hl", query.astype(jnp.float32), null_key.reshape(heads, HD)) * scale
    )
    masked = jnp.where(usable[None, None, :], scores, -1e30)
    highest = jnp.maximum(jnp.max(masked, axis=-1), null_scores)
    expo = jnp.where(usable[None, None, :], jnp.exp(masked - highest[:, :, None]), 0.0)
    null_expo = jnp.exp(null_scores - highest)
    denom = jnp.sum(expo, axis=-1) + null_expo
    weights = (expo / denom[:, :, None]).astype(jnp.bfloat16)
    null_weights = (null_expo / denom).astype(jnp.bfloat16)
    summed = jnp.einsum("hls,shd->lhd", weights, valset, preferred_element_type=jnp.float32)
    summed = (
        summed
        + jnp.transpose(null_weights.astype(jnp.float32))[:, :, None]
        * null_value.reshape(heads, HD)[None, :, :]
    )
    return summed.reshape(count, width).astype(jnp.bfloat16)


def local(
    audio_rows,
    routing,
    row_band,
    block_band,
    latents,
    kv_weight,
    null_key,
    null_value,
    out_weight,
    mlp_gain,
    up_weight,
    down_weight,
):
    local_rows = audio_rows.shape[0]
    owners = lax.axis_size("tm")
    capacity = max(2, 2 * local_rows // owners)
    destination = routing[:, 0]
    onehot = (destination[:, None] == jnp.arange(owners, dtype=jnp.int32)[None, :]).astype(
        jnp.int32
    )
    slot_index = jnp.sum((jnp.cumsum(onehot, axis=0) - onehot) * onehot, axis=1)
    band_send = (
        jnp.full((owners, capacity), -4, jnp.int32).at[destination, slot_index].set(row_band)
    )
    payload = (
        jnp.zeros((owners, capacity, audio_rows.shape[1]), jnp.bfloat16)
        .at[destination, slot_index]
        .set(audio_rows)
    )
    frame_recv, band_recv = (
        lax.all_to_all(payload, "tm", split_axis=0, concat_axis=0, tiled=True),
        lax.all_to_all(band_send, "tm", split_axis=0, concat_axis=0, tiled=True),
    )
    frame_slots = frame_recv.reshape(owners * capacity, audio_rows.shape[1])
    kv_whole = lax.all_gather(kv_weight, "tm", axis=0, tiled=True)
    kv_slots = jnp.dot(frame_slots, kv_whole, preferred_element_type=jnp.float32).astype(
        jnp.bfloat16
    )
    usable = jnp.abs(band_recv.reshape(-1) - block_band[0]) <= 1
    attended = attend(latents, kv_slots, usable, null_key, null_value)
    joined = (
        latents.astype(jnp.float32)
        + jnp.dot(attended, out_weight, preferred_element_type=jnp.float32)
    ).astype(jnp.bfloat16)
    window = lax.all_gather(joined, "grp", axis=0, tiled=True)
    values = window.astype(jnp.float32)
    center = values - jnp.mean(values, axis=-1, keepdims=True)
    spread = jnp.mean(center * center, axis=-1, keepdims=True)
    normed = (center * lax.rsqrt(spread + 1e-05) * mlp_gain).astype(jnp.bfloat16)
    up_whole = lax.all_gather(up_weight, "tm", axis=0, tiled=True)
    hidden = jax.nn.gelu(jnp.dot(normed, up_whole, preferred_element_type=jnp.float32)).astype(
        jnp.bfloat16
    )
    down_whole = lax.all_gather(down_weight, "tm", axis=1, tiled=True)
    partial_terms = jnp.dot(hidden, down_whole, preferred_element_type=jnp.float32)
    summed = lax.psum_scatter(
        partial_terms.astype(jnp.bfloat16), "grp", scatter_dimension=1, tiled=True
    ).astype(jnp.float32)
    columns = summed.shape[1]
    residual = lax.dynamic_slice_in_dim(window, lax.axis_index("grp") * columns, columns, 1)
    return (residual.astype(jnp.float32) + summed).astype(jnp.bfloat16)


def solution(mesh):
    return jax.shard_map(
        local,
        mesh=mesh,
        in_specs=(
            P(("grp", "tm"), None),
            P(("grp", "tm"), None),
            P(("grp", "tm")),
            P(("grp", "tm")),
            P(("grp", "tm"), None),
            P("tm", None),
            P(),
            P(),
            P(),
            P(),
            P("tm", "grp"),
            P("grp", "tm"),
        ),
        out_specs=P("tm", "grp"),
        check_vma=False,
    )
```

profile of v0, /device:TPU:4, one launch (start us, length us, event | category | flops | bytes accessed | tf_op | source)
XLA Modules:
  0.0 409.4 jit_solution(6860306548943538803)
XLA Ops:
  6.5 0.7 all-gather.5.cloned.1.call-update
  7.3 0.7 fusion.51
  8.0 0.6 reduce-window.6
  8.8 0.8 fusion.50
  9.6 0.7 or_select_fusion
  10.3 21.2 %scatter_fusion.1 = s32[64,8]{0,1:T(8,128)S(1)} fusion(s32[64,8]{0,1:T(8,128)S(1)} %broadcast_in_dim.40, s32[256]{0:T(256)S(1)} %bitcast.106, s32[256]{0:T(256)} %param.14), kind=kCustom, calls=%fused_computation.1 | custom fusion | bytes 5120 | tf_op jit(solution)/shard_map/scatter | solution.py:61
  31.6 0.7 copy.24
  32.3 13.8 %all-to-all-start.1 = ((s32[64,1,8]{2,1,0:T(1,128)}), s32[64,1,8]{2,1,0:T(1,128)S(1)}, u32[]{:S(2)}, u32[]{:S(2)}) async-start(s32[64,1,8]{2,1,0:T(1,128)} %copy.24), calls=%async_computation.1 | async-start | bytes 65536 | tf_op jit(solution)/shard_map/all_to_all | solution.py:70
  46.1 1.1 broadcast_in_dim.39
  47.2 36.1 %scatter_fusion = bf16[64,8,1024]{2,1,0:T(8,128)(2,1)} fusion(bf16[64,8,1024]{2,1,0:T(8,128)(2,1)} %broadcast_in_dim.39, s32[256]{0:T(256)S(1)} %bitcast.107, bf16[256,1024]{1,0:T(8,128)(2,1)S(1)} %copy-done.3), kind=kCustom, calls=%fused_computation | custom fusion | bytes 1574912 | tf_op jit(solution)/shard_map/scatter | solution.py:66
  83.4 10.6 %all-to-all-start = ((bf16[64,8,1024]{2,1,0:T(8,128)(2,1)}), bf16[64,8,1024]{2,1,0:T(8,128)(2,1)S(1)}, u32[]{:S(2)}, u32[]{:S(2)}) async-start(bf16[64,8,1024]{2,1,0:T(8,128)(2,1)} %scatter_fusion), calls=%async_computation | async-start | bytes 2097152 | tf_op jit(solution)/shard_map/all_to_all | solution.py:69
  94.8 0.2 fusion.43
  95.3 27.6 %all-to-all-done = bf16[64,8,1024]{2,1,0:T(8,128)(2,1)S(1)} async-done(((bf16[64,8,1024]{2,1,0:T(8,128)(2,1)}), bf16[64,8,1024]{2,1,0:T(8,128)(2,1)S(1)}, u32[]{:S(2)}, u32[]{:S(2)}) %all-to-all-start) | async-done | bytes 1048608 | tf_op jit(solution)/shard_map/all_to_all | solution.py:69
  122.8 4.5 %convolution_convert_fusion = bf16[512,2048]{1,0:T(8,128)(2,1)S(1)} fusion(bf16[1024,2048]{1,0:T(8,128)(2,1)} %all-gather.5.cloned.1.call-done, bf16[64,8,1024]{2,1,0:T(8,128)(2,1)S(1)} %all-to-all-done), kind=kOutput, calls=%fused_computation.18 | convolution fusion | flops 2148532224 | bytes 7340032 | tf_op jit(solution)/shard_map/dot_general | solution.py:74
  127.6 0.5 bitcast_reduce_fusion
  128.1 1.3 copy-done.2
  129.4 0.6 fusion.29
  130.1 1.3 copy.32
  131.4 2.9 fusion.31
  134.3 1.2 fusion.32
  135.6 0.7 all-gather.11.cloned.1.call-update
  136.3 0.5 all-gather.9.cloned.1.call-update
  137.1 38.1 %all-gather.7.cloned.1.call-done = bf16[1024,1024]{1,0:T(8,128)(2,1)} async-done(((bf16[128,1024]{1,0:T(8,128)(2,1)}), bf16[1024,1024]{1,0:T(8,128)(2,1)}) %all-gather.7.cloned.1.call-update) | async-done | bytes 2097168 | tf_op jit(solution)/shard_map/all_gather | solution.py:83
  175.2 2.1 convert_reduce_fusion
  177.4 0.7 fusion.2
  178.2 81.9 %all-gather.11.cloned.1.call-done = bf16[1024,1024]{0,1:T(8,128)(2,1)} async-done(((bf16[1024,16]{0,1:T(8,128)(2,1)}), bf16[1024,1024]{0,1:T(8,128)(2,1)}) %all-gather.11.cloned.1.call-update) | async-done | bytes 2097168 | tf_op jit(solution)/shard_map/all_gather | solution.py:92
  260.0 83.9 %all-gather.9.cloned.1.call-done = bf16[1024,1024]{1,0:T(8,128)(2,1)} async-done(((bf16[16,1024]{1,0:T(8,128)(2,1)}), bf16[1024,1024]{1,0:T(8,128)(2,1)}) %all-gather.9.cloned.1.call-update) | async-done | bytes 2097168 | tf_op jit(solution)/shard_map/all_gather | solution.py:88
  343.9 8.8 %fusion.26 = bf16[1024,1024]{1,0:T(8,128)(2,1)} fusion(bf16[1024,1024]{0,1:T(8,128)(2,1)} %all-gather.11.cloned.1.call-done, bf16[1024,1024]{1,0:T(8,128)(2,1)} %all-gather.9.cloned.1.call-done, bf16[1024,1024]{1,0:T(8,128)(2,1)} %all-gather.7.cloned.1.call-done, f32[1024]{0:T(1024)S(1)} %copy-done.7, f32[1024]{0:T(1024)S(1)} %add_rsqrt_fusion, ...), kind=kOutput, calls=%fused_computation.34 | convolution fusion | flops 4310695936 | bytes 8400896 | tf_op jit(solution)/shard_map/dot_general | solution.py:93
  352.7 3.9 copy.33
  356.7 43.3 %reduce-scatter.4.cloned.1.call-done = bf16[128,1024]{1,0:T(8,128)(2,1)} async-done(((bf16[1024,1024]{1,0:T(8,128)(2,1)}), bf16[128,1024]{1,0:T(8,128)(2,1)}) %reduce-scatter.4.cloned.1.call-update) | async-done | bytes 262160
  400.0 1.1 copy.34
  401.1 1.7 add_convert_fusion
  (36 shorter events, 1.3 us)
Async XLA Ops:
  6.5 127.8 %copy-start = (bf16[1024,1024]{1,0:T(8,128)(2,1)S(1)}, bf16[1024,1024]{1,0:T(8,128)(2,1)}, u32[]{:S(2)}) copy-start(bf16[1024,1024]{1,0:T(8,128)(2,1)} %param.20) | copy-start | bytes 6291460
  6.5 40.7 %copy-start.3 = (bf16[256,1024]{1,0:T(8,128)(2,1)S(1)}, bf16[256,1024]{1,0:T(8,128)(2,1)}, u32[]{:S(2)}) copy-start(bf16[256,1024]{1,0:T(8,128)(2,1)} %param.12) | copy-start | bytes 1572868
  6.5 116.3 %all-gather.5.cloned.1.call-start = ((), (), s32[]{:S(2)}) async-start(), calls=%async_computation.3 | async-start | bytes 4259840 | tf_op jit(solution)/shard_map/all_gather | solution.py:73
  32.3 51.1 %all-to-all-start.1 = ((s32[64,1,8]{2,1,0:T(1,128)}), s32[64,1,8]{2,1,0:T(1,128)S(1)}, u32[]{:S(2)}, u32[]{:S(2)}) async-start(s32[64,1,8]{2,1,0:T(1,128)} %copy.24), calls=%async_computation.1 | async-start | bytes 65536 | tf_op jit(solution)/shard_map/all_to_all | solution.py:70
  83.4 11.4 %copy-start.4 = (bf16[128,1024]{1,0:T(8,128)(2,1)S(1)}, bf16[128,1024]{1,0:T(8,128)(2,1)}, u32[]{:S(2)}) copy-start(bf16[128,1024]{1,0:T(8,128)(2,1)} %param.16) | copy-start | bytes 786436
  83.4 11.4 %copy-start.5 = (f32[1024]{0:T(1024)S(1)}, f32[1024]{0:T(1024)}, u32[]{:S(2)}) copy-start(f32[1024]{0:T(1024)} %param.18) | copy-start | bytes 12292
  83.4 39.4 %all-to-all-start = ((bf16[64,8,1024]{2,1,0:T(8,128)(2,1)}), bf16[64,8,1024]{2,1,0:T(8,128)(2,1)S(1)}, u32[]{:S(2)}, u32[]{:S(2)}) async-start(bf16[64,8,1024]{2,1,0:T(8,128)(2,1)} %scatter_fusion), calls=%async_computation | async-start | bytes 2097152 | tf_op jit(solution)/shard_map/all_to_all | solution.py:69
  94.0 81.2 %all-gather.7.cloned.1.call-start = ((), (), s32[]{:S(2)}) async-start(), calls=%async_computation.4 | async-start | bytes 2359296 | tf_op jit(solution)/shard_map/all_gather | solution.py:83
  128.1 1.4 copy-start.2
  129.4 2.0 copy-start.6
  135.5 124.5 %all-gather.11.cloned.1.call-start = ((), (), s32[]{:S(2)}) async-start(), calls=%async_computation.6 | async-start | bytes 2129920 | tf_op jit(solution)/shard_map/all_gather | solution.py:92
  136.3 207.6 %all-gather.9.cloned.1.call-start = ((), (), s32[]{:S(2)}) async-start(), calls=%async_computation.5 | async-start | bytes 2129920 | tf_op jit(solution)/shard_map/all_gather | solution.py:88
  136.8 207.1 %copy-start.7 = (f32[1024]{0:T(1024)S(1)}, f32[1024]{0:T(1024)}, u32[]{:S(2)}) copy-start(f32[1024]{0:T(1024)} %param.21) | copy-start | bytes 12292
  136.9 263.1 %reduce-scatter.4.cloned.1.call-start = ((), (), s32[]{:S(2)}) async-start(), calls=%async_computation.7 | async-start | bytes 2359296
  175.2 2.2 copy-start.1
Sparse Core Ops, SparseCore 0:
  10.7 88.6 all-gather.4
  135.7 39.5 all-gather.6
  178.6 81.3 all-gather.10
  263.2 80.6 all-gather.8
  356.8 43.1 reduce-scatter.3
where the time goes:
time: 411 us; the launch traced here: 409 us
  waiting for transfers between devices  277 us (67%)
  local copies, waits for them, and re-layouts  67.6 us (16%)
  starting transfers between devices  24.8 us (6%)
  matrix products  18.1 us (4%)
  between operations  13.9 us (3%)
  other arithmetic  8.18 us (2%)
    all_gather x1, waiting for transfers between devices, local(): up_whole = lax.all_gather(up_weight, 'tm', axis=0, tiled=True)  83.9 us
    all_gather x1, waiting for transfers between devices, local(): down_whole = lax.all_gather(down_weight, 'tm', axis=1, tiled=True)  81.9 us
    unnamed x6, waiting for transfers between devices  45.3 us
    all_gather x1, waiting for transfers between devices, local(): window = lax.all_gather(joined, 'grp', axis=0, tiled=True)  38.1 us
    scatter x1, local copies, waits for them, and re-layouts, local(): payload = jnp.zeros((owners, capacity, audio_rows.shape[1]), jnp.bfloat16...  36.1 us
    all_to_all x1, waiting for transfers between devices, local(): lax.all_to_all(payload, 'tm', split_axis=0, concat_axis=0, tiled=True)  27.6 us
    scatter x1, local copies, waits for them, and re-layouts, local(): jnp.full((owners, capacity), -4, jnp.int32).at[destination, slot_index]  21.2 us
    all_to_all x1, starting transfers between devices, local(): lax.all_to_all(band_send, 'tm', split_axis=0, concat_axis=0, tiled=True)  13.8 us
  transfers between devices with their start and end apart: 7, of which 5 were waited for; matrix products, arithmetic and copies ran while one was open for 16% of the time, Pallas kernels for 0%

commit v1 on v0

--- a/solution.py
+++ b/solution.py
@@ -89,7 +89,9 @@
     hidden = jax.nn.gelu(jnp.dot(normed, up_whole, preferred_element_type=jnp.float32)).astype(
         jnp.bfloat16
     )
-    down_whole = lax.all_gather(down_weight, "tm", axis=1, tiled=True)
+    down_whole = jnp.concatenate(
+        lax.all_to_all(jnp.stack([down_weight] * lax.axis_size("tm")), "tm", 0, 0), axis=1
+    )
     partial_terms = jnp.dot(hidden, down_whole, preferred_element_type=jnp.float32)
     summed = lax.psum_scatter(
         partial_terms.astype(jnp.bfloat16), "grp", scatter_dimension=1, tiled=True

time: 411 us -> 328 us (0.80)
  the two profiles are of different devices: /device:TPU:4 before, /device:TPU:2 now
where the time goes in v1:
time: 328 us; the launch traced here: 326 us
  waiting for transfers between devices  185 us (56%)
  local copies, waits for them, and re-layouts  69.2 us (21%)
  starting transfers between devices  30.9 us (9%)
  matrix products  18.2 us (6%)
  between operations  14 us (4%)
  other arithmetic  8.18 us (2%)
    all_gather x1, waiting for transfers between devices, local(): up_whole = lax.all_gather(up_weight, 'tm', axis=0, tiled=True)  65.9 us
    unnamed x5, waiting for transfers between devices  44.7 us
    scatter x1, local copies, waits for them, and re-layouts, local(): payload = jnp.zeros((owners, capacity, audio_rows.shape[1]), jnp.bfloat16...  36.1 us
    all_gather x1, waiting for transfers between devices, local(): window = lax.all_gather(joined, 'grp', axis=0, tiled=True)  31 us
    all_to_all x1, waiting for transfers between devices, local(): lax.all_to_all(payload, 'tm', split_axis=0, concat_axis=0, tiled=True)  27.4 us
    scatter x1, local copies, waits for them, and re-layouts, local(): jnp.full((owners, capacity), -4, jnp.int32).at[destination, slot_index]  21.2 us
    all_to_all x1, waiting for transfers between devices, local(): lax.all_to_all(jnp.stack([down_weight] * lax.axis_size('tm')), 'tm', 0, 0)  16.3 us
    all_to_all x1, starting transfers between devices, local(): lax.all_to_all(band_send, 'tm', split_axis=0, concat_axis=0, tiled=True)  13.9 us
  transfers between devices with their start and end apart: 7, of which 5 were waited for; matrix products, arithmetic and copies ran while one was open for 21% of the time, Pallas kernels for 0%

profile of v1, /device:TPU:2, one launch (start us, length us, event | category | flops | bytes accessed | tf_op | source)
XLA Modules:
  0.0 325.6 jit_solution(16900585770056066666)
XLA Ops:
  6.5 0.7 all-gather.4.cloned.1.call-update
  7.3 0.7 fusion.51
  8.0 0.6 reduce-window.6
  8.8 0.8 fusion.50
  9.6 0.7 or_select_fusion
  10.3 21.2 %scatter_fusion.1 = s32[64,8]{0,1:T(8,128)S(1)} fusion(s32[64,8]{0,1:T(8,128)S(1)} %broadcast_in_dim.40, s32[256]{0:T(256)S(1)} %bitcast.109, s32[256]{0:T(256)} %param.14), kind=kCustom, calls=%fused_computation.1 | custom fusion | bytes 5120 | tf_op jit(solution)/shard_map/scatter | solution.py:61
  31.6 0.7 copy.25
  32.3 13.9 %all-to-all-start.1 = ((s32[64,1,8]{2,1,0:T(1,128)}), s32[64,1,8]{2,1,0:T(1,128)S(1)}, u32[]{:S(2)}, u32[]{:S(2)}) async-start(s32[64,1,8]{2,1,0:T(1,128)} %copy.25), calls=%async_computation.1 | async-start | bytes 65536 | tf_op jit(solution)/shard_map/all_to_all | solution.py:70
  46.2 1.1 broadcast_in_dim.39
  47.3 36.1 %scatter_fusion = bf16[64,8,1024]{2,1,0:T(8,128)(2,1)} fusion(bf16[64,8,1024]{2,1,0:T(8,128)(2,1)} %broadcast_in_dim.39, s32[256]{0:T(256)S(1)} %bitcast.110, bf16[256,1024]{1,0:T(8,128)(2,1)S(1)} %copy-done.3), kind=kCustom, calls=%fused_computation | custom fusion | bytes 1574912 | tf_op jit(solution)/shard_map/scatter | solution.py:66
  83.4 10.7 %all-to-all-start = ((bf16[64,8,1024]{2,1,0:T(8,128)(2,1)}), bf16[64,8,1024]{2,1,0:T(8,128)(2,1)S(1)}, u32[]{:S(2)}, u32[]{:S(2)}) async-start(bf16[64,8,1024]{2,1,0:T(8,128)(2,1)} %scatter_fusion), calls=%async_computation | async-start | bytes 2097152 | tf_op jit(solution)/shard_map/all_to_all | solution.py:69
  95.3 27.4 %all-to-all-done = bf16[64,8,1024]{2,1,0:T(8,128)(2,1)S(1)} async-done(((bf16[64,8,1024]{2,1,0:T(8,128)(2,1)}), bf16[64,8,1024]{2,1,0:T(8,128)(2,1)S(1)}, u32[]{:S(2)}, u32[]{:S(2)}) %all-to-all-start) | async-done | bytes 1048608 | tf_op jit(solution)/shard_map/all_to_all | solution.py:69
  122.7 4.5 %convolution_convert_fusion = bf16[512,2048]{1,0:T(8,128)(2,1)S(1)} fusion(bf16[1024,2048]{1,0:T(8,128)(2,1)} %all-gather.4.cloned.1.call-done, bf16[64,8,1024]{2,1,0:T(8,128)(2,1)S(1)} %all-to-all-done), kind=kOutput, calls=%fused_computation.18 | convolution fusion | flops 2148532224 | bytes 7340032 | tf_op jit(solution)/shard_map/dot_general | solution.py:74
  127.4 0.5 bitcast_reduce_fusion
  127.9 1.3 copy-done.2
  129.3 0.6 fusion.29
  129.9 1.3 copy.33
  131.3 2.9 fusion.31
  134.2 1.2 fusion.32
  135.4 1.6 stack.2
  137.0 6.0 %all-to-all-start.2 = ((bf16[64,1024,16]{1,2,0:T(8,128)(2,1)}), bf16[64,1024,16]{1,2,0:T(8,128)(2,1)}, u32[]{:S(2)}, u32[]{:S(2)}) async-start(bf16[64,1024,16]{1,2,0:T(8,128)(2,1)} %stack.2), calls=%async_computation.2 | async-start | bytes 4194304 | tf_op jit(solution)/shard_map/all_to_all | solution.py:93
  143.1 0.7 all-gather.8.cloned.1.call-update
  144.0 31.0 %all-gather.6.cloned.1.call-done = bf16[1024,1024]{1,0:T(8,128)(2,1)} async-done(((bf16[128,1024]{1,0:T(8,128)(2,1)}), bf16[1024,1024]{1,0:T(8,128)(2,1)}) %all-gather.6.cloned.1.call-update) | async-done | bytes 2097168 | tf_op jit(solution)/shard_map/all_gather | solution.py:83
  175.0 2.1 convert_reduce_fusion
  177.2 0.7 fusion.2
  177.9 16.3 %all-to-all-done.2 = bf16[64,1024,16]{1,2,0:T(8,128)(2,1)} async-done(((bf16[64,1024,16]{1,2,0:T(8,128)(2,1)}), bf16[64,1024,16]{1,2,0:T(8,128)(2,1)}, u32[]{:S(2)}, u32[]{:S(2)}) %all-to-all-start.2) | async-done | bytes 2097184 | tf_op jit(solution)/shard_map/all_to_all | solution.py:93
  194.2 65.9 %all-gather.8.cloned.1.call-done = bf16[1024,1024]{1,0:T(8,128)(2,1)} async-done(((bf16[16,1024]{1,0:T(8,128)(2,1)}), bf16[1024,1024]{1,0:T(8,128)(2,1)}) %all-gather.8.cloned.1.call-update) | async-done | bytes 2097168 | tf_op jit(solution)/shard_map/all_gather | solution.py:88
  260.1 8.8 %fusion.26 = bf16[1024,1024]{1,0:T(8,128)(2,1)} fusion(bf16[1024,1024]{0,1:T(8,128)(2,1)} %bitcast.22, bf16[1024,1024]{1,0:T(8,128)(2,1)} %all-gather.8.cloned.1.call-done, bf16[1024,1024]{1,0:T(8,128)(2,1)} %all-gather.6.cloned.1.call-done, f32[1024]{0:T(1024)S(1)} %copy-done.8, f32[1024]{0:T(1024)S(1)} %add_rsqrt_fusion, f32[1024]{0:T(1024)S(1)} %broadcast_multiply_fusion), kind=kOutput, calls=%fused_computation.34 | convolution fusion | flops 4310695936 | bytes 8400896 | tf_op jit(solution)/shard_map/dot_general | solution.py:95
  268.9 4.0 %copy.34 = bf16[1024,1024]{0,1:T(8,128)(2,1)} copy(bf16[1024,1024]{1,0:T(8,128)(2,1)} %fusion.26) | data formatting | bytes 4194304
  272.9 43.2 %reduce-scatter.4.cloned.1.call-done = bf16[128,1024]{1,0:T(8,128)(2,1)} async-done(((bf16[1024,1024]{1,0:T(8,128)(2,1)}), bf16[128,1024]{1,0:T(8,128)(2,1)}) %reduce-scatter.4.cloned.1.call-update) | async-done | bytes 262160
  316.2 1.1 copy.35
  317.3 1.7 add_convert_fusion
  (38 shorter events, 1.5 us)
Async XLA Ops:
  6.5 127.6 %copy-start = (bf16[1024,1024]{1,0:T(8,128)(2,1)S(1)}, bf16[1024,1024]{1,0:T(8,128)(2,1)}, u32[]{:S(2)}) copy-start(bf16[1024,1024]{1,0:T(8,128)(2,1)} %param.20) | copy-start | bytes 6291460
  6.5 40.7 %copy-start.3 = (bf16[256,1024]{1,0:T(8,128)(2,1)S(1)}, bf16[256,1024]{1,0:T(8,128)(2,1)}, u32[]{:S(2)}) copy-start(bf16[256,1024]{1,0:T(8,128)(2,1)} %param.12) | copy-start | bytes 1572868
  6.5 116.1 %all-gather.4.cloned.1.call-start = ((), (), s32[]{:S(2)}) async-start(), calls=%async_computation.4 | async-start | bytes 4259840 | tf_op jit(solution)/shard_map/all_gather | solution.py:73
  32.3 51.1 %all-to-all-start.1 = ((s32[64,1,8]{2,1,0:T(1,128)}), s32[64,1,8]{2,1,0:T(1,128)S(1)}, u32[]{:S(2)}, u32[]{:S(2)}) async-start(s32[64,1,8]{2,1,0:T(1,128)} %copy.25), calls=%async_computation.1 | async-start | bytes 65536 | tf_op jit(solution)/shard_map/all_to_all | solution.py:70
  83.4 11.4 %copy-start.4 = (bf16[128,1024]{1,0:T(8,128)(2,1)S(1)}, bf16[128,1024]{1,0:T(8,128)(2,1)}, u32[]{:S(2)}) copy-start(bf16[128,1024]{1,0:T(8,128)(2,1)} %param.16) | copy-start | bytes 786436
  83.4 11.4 %copy-start.6 = (f32[1024]{0:T(1024)S(1)}, f32[1024]{0:T(1024)}, u32[]{:S(2)}) copy-start(f32[1024]{0:T(1024)} %param.18) | copy-start | bytes 12292
  83.4 39.3 %all-to-all-start = ((bf16[64,8,1024]{2,1,0:T(8,128)(2,1)}), bf16[64,8,1024]{2,1,0:T(8,128)(2,1)S(1)}, u32[]{:S(2)}, u32[]{:S(2)}) async-start(bf16[64,8,1024]{2,1,0:T(8,128)(2,1)} %scatter_fusion), calls=%async_computation | async-start | bytes 2097152 | tf_op jit(solution)/shard_map/all_to_all | solution.py:69
  94.1 80.9 %all-gather.6.cloned.1.call-start = ((), (), s32[]{:S(2)}) async-start(), calls=%async_computation.5 | async-start | bytes 2359296 | tf_op jit(solution)/shard_map/all_gather | solution.py:83
  127.9 1.4 copy-start.2
  129.3 2.0 copy-start.7
  134.2 1.2 copy-start.5
  137.0 57.2 %all-to-all-start.2 = ((bf16[64,1024,16]{1,2,0:T(8,128)(2,1)}), bf16[64,1024,16]{1,2,0:T(8,128)(2,1)}, u32[]{:S(2)}, u32[]{:S(2)}) async-start(bf16[64,1024,16]{1,2,0:T(8,128)(2,1)} %stack.2), calls=%async_computation.2 | async-start | bytes 4194304 | tf_op jit(solution)/shard_map/all_to_all | solution.py:93
  143.0 117.1 %all-gather.8.cloned.1.call-start = ((), (), s32[]{:S(2)}) async-start(), calls=%async_computation.6 | async-start | bytes 2129920 | tf_op jit(solution)/shard_map/all_gather | solution.py:88
  143.8 116.3 %copy-start.8 = (f32[1024]{0:T(1024)S(1)}, f32[1024]{0:T(1024)}, u32[]{:S(2)}) copy-start(f32[1024]{0:T(1024)} %param.21) | copy-start | bytes 12292
  143.8 172.4 %reduce-scatter.4.cloned.1.call-start = ((), (), s32[]{:S(2)}) async-start(), calls=%async_computation.7 | async-start | bytes 2359296
  175.0 2.2 copy-start.1
Sparse Core Ops, SparseCore 0:
  10.7 89.1 all-gather.3
  135.5 39.4 all-gather.5
  178.3 81.7 all-gather.7
  273.0 43.0 reduce-scatter.3
